TPU v7x, 256 devices: a whole 4x4x8 slice. The times are simulated.
256 devices in a mesh: req: 32 (over z_lo, x, y), tp: 8 (over z_hi, core).
Axes of the slice: x: 4, y: 4, z: 8 (z_hi: 4, z_lo: 2; z = z_hi * 2 + z_lo), core: 2. Of those that a mesh axis runs over, the one named last changes fastest.
Arguments:
- queries: bfloat16 [32768, 5120], P('req', 'tp')
- keys: bfloat16 [32768, 5120], P('req', 'tp')
- values: bfloat16 [32768, 5120], P('req', 'tp'), may hold values from -6 to 6
- cross_queries: bfloat16 [32768, 5120], P('req', 'tp')
- text_kv: bfloat16 [1024, 2, 5120], P(('req', 'tp'))
- segment_ids: int32 [32, 1024], P('req'), may hold values from 0 to 5, never falling along the last dimension, each value on 1 to 682 neighbouring positions
- prompt_of: int32 [32], P('req'), may hold values from 0 to 1
- page_owner: int32 [2048, 1], P('req'), may hold values from 0 to 31; in each aligned block of 64 rows (0 to 63, 64 to 127, ...) at most 3 rows name the same one
Outputs:
- self_out: bfloat16 [32768, 5120], P('req', 'tp')
- cross_out: bfloat16 [32768, 5120], P('req', 'tp')
- cache: bfloat16 [49152, 2, 5120], P('req', None, 'tp')
Inputs may be any that keep to these rules, and one draw needn't show every extreme that they name: `page_owner`: among the pages of one stream (an aligned block of 64 rows), no device index appears more than 3 times; in some streams one appears exactly 3 times.
All inputs are finite; a program needn't handle non-finite values.
Results may differ from a plain program's by a relative error of at most 0.003.
The roundings to bfloat16 on the way count: a program that leaves them out, or rounds other values in their place, can miss the bound.
Values may be sent and summed in bfloat16 or wider, within the bound.
A program may use at most 128 MiB of HBM per device.

v0:
```python
import math
import jax
import jax.numpy as jnp
from jax import lax
from jax.sharding import PartitionSpec as P

HEADS = 40
HEAD = 128
TEXT = 512
PAGE = 16
EPSILON = 1e-06
NEGATIVE = -1e30


def square_sums(block):
    wide = block.astype(jnp.float32)
    return jnp.sum(wide * wide, axis=1)


def scaled_rows(block, totals, width):
    factor = lax.rsqrt(totals / width + EPSILON)
    return (block.astype(jnp.float32) * factor[:, None]).astype(jnp.bfloat16)


def empty_state(heads, count, depth):
    return (
        jnp.full((heads, count), NEGATIVE, jnp.float32),
        jnp.zeros((heads, count), jnp.float32),
        jnp.zeros((heads, count, depth), jnp.float32),
    )


def blend(state, scores, allowed, value_part):
    running_max, running_sum, accum = state
    masked = jnp.where(allowed, scores, NEGATIVE)
    new_max = jnp.maximum(running_max, jnp.max(masked, axis=2))
    weights = jnp.where(allowed, jnp.exp(masked - new_max[:, :, None]), 0.0)
    new_sum = jnp.sum(weights, axis=2)
    product = jnp.einsum(
        "hqk,khe->hqe", weights.astype(jnp.bfloat16), value_part, preferred_element_type=jnp.float32
    )
    return (new_max, new_sum, product)


def finish(state):
    return state[2] / state[1][:, :, None]


def attend_block(state, query_part, query_seg, key_part, value_part, key_seg, scale):
    scores = (
        jnp.einsum("qhe,khe->hqk", query_part, key_part, preferred_element_type=jnp.float32) * scale
    )
    allowed = (query_seg[:, None] == key_seg[None, :])[None]
    return blend(state, scores, allowed, value_part)


def self_attention(query_heads, key_heads, value_heads, segments):
    length, heads, depth = query_heads.shape
    block = math.gcd(length, 512)
    scale = depth ** (-0.5)
    results = []
    for query_start in range(0, length, block):
        query_part = query_heads[query_start : query_start + block]
        query_seg = segments[query_start : query_start + block]
        state = empty_state(heads, block, depth)
        state = attend_block(state, query_part, query_seg, key_heads, value_heads, segments, scale)
        results.append(finish(state))
    joined = jnp.concatenate(results, axis=1)
    return joined.transpose(1, 0, 2).reshape(length, heads * depth).astype(jnp.bfloat16)


def cross_attention(cross_heads, prompt_rows):
    length, heads, depth = cross_heads.shape
    count = prompt_rows.shape[0]
    key_part = prompt_rows[:, 0, :].reshape(count, heads, depth)
    value_part = prompt_rows[:, 1, :].reshape(count, heads, depth)
    block = math.gcd(length, 512)
    scale = depth ** (-0.5)
    everywhere = jnp.ones((1, 1, count), dtype=jnp.bool_)
    results = []
    for query_start in range(0, length, block):
        query_part = cross_heads[query_start : query_start + block]
        scores = (
            jnp.einsum("qhe,khe->hqk", query_part, key_part, preferred_element_type=jnp.float32)
            * scale
        )
        state = blend(empty_state(heads, block, depth), scores, everywhere, value_part)
        results.append(finish(state))
    joined = jnp.concatenate(results, axis=1)
    return joined.transpose(1, 0, 2).reshape(length, heads * depth).astype(jnp.bfloat16)


def per_device(queries, keys, values, cross_queries, text_kv, segment_ids, prompt_of, page_owner):
    width = HEADS * HEAD
    stream = queries.shape[0]
    width_dev = queries.shape[1]
    heads_dev = width_dev // HEAD
    query_total, key_total, cross_total = lax.psum(
        (square_sums(queries), square_sums(keys), square_sums(cross_queries)), "tp"
    )
    query_hat = scaled_rows(queries, query_total, width)
    key_hat = scaled_rows(keys, key_total, width)
    cross_hat = scaled_rows(cross_queries, cross_total, width)
    text_keys = text_kv[:, 0, :]
    text_hat = scaled_rows(text_keys, square_sums(text_keys), width)
    text_ready = jnp.stack([text_hat, text_kv[:, 1, :]], axis=1)
    nreq = lax.axis_size("req")
    pages = stream // PAGE
    capacity = max(2, (3 * pages + 2 * nreq - 1) // (2 * nreq))
    owners = page_owner[:, 0]
    same_owner = owners[:, None] == owners[None, :]
    before = lax.broadcasted_iota(jnp.int32, (pages, pages), 1) < lax.broadcasted_iota(
        jnp.int32, (pages, pages), 0
    )
    rank = jnp.sum(jnp.where(jnp.logical_and(same_owner, before), 1, 0), axis=1).astype(jnp.int32)
    slot_index = owners * capacity + rank
    picker = (
        lax.broadcasted_iota(jnp.int32, (nreq * capacity, pages), 0) == slot_index[None, :]
    ).astype(jnp.bfloat16)
    page_data = jnp.stack([key_hat, values], axis=1).reshape(pages, PAGE * 2 * width_dev)
    outgoing = jnp.dot(picker, page_data, preferred_element_type=jnp.float32).astype(jnp.bfloat16)
    outgoing = outgoing.reshape(nreq * capacity * PAGE, 2, width_dev)
    cache = lax.all_to_all(outgoing, "req", split_axis=0, concat_axis=0, tiled=True)
    query_heads = query_hat.reshape(stream, heads_dev, HEAD)
    key_heads = key_hat.reshape(stream, heads_dev, HEAD)
    value_heads = values.reshape(stream, heads_dev, HEAD)
    self_out = self_attention(query_heads, key_heads, value_heads, segment_ids[0])
    cross_heads = cross_hat.reshape(stream, heads_dev, HEAD)
    prompt_start = prompt_of[0] * TEXT
    gathered = lax.all_gather(text_ready, ("req", "tp"), axis=0, tiled=True)
    prompt_rows = lax.dynamic_slice_in_dim(gathered, prompt_start, TEXT, 0)
    head_start = lax.axis_index("tp") * width_dev
    prompt_rows = lax.dynamic_slice_in_dim(prompt_rows, head_start, width_dev, 2)
    cross_out = cross_attention(cross_heads, prompt_rows)
    return (self_out, cross_out, cache)


def solution(mesh):
    placed = (
        P("req", "tp"),
        P("req", "tp"),
        P("req", "tp"),
        P("req", "tp"),
        P(("req", "tp"), None, None),
        P("req", None),
        P("req"),
        P("req", None),
    )
    return jax.shard_map(
        per_device,
        mesh=mesh,
        in_specs=placed,
        out_specs=(P("req", "tp"), P("req", "tp"), P("req", None, "tp")),
        check_vma=False,
    )
```

profile of v0, /device:TPU:64, one launch (start us, length us, event | category | flops | bytes accessed | tf_op | source)
XLA Modules:
  0.0 517.8 jit_solution(12269761902777181673)
XLA Ops:
  7.2 0.0 copy-start.3
  7.2 0.0 all-gather.2.cloned.1.call-start
  7.2 1.2 fusion.52
  8.4 0.2 fusion.38
  8.6 0.1 fusion.39
  8.7 0.1 pad_maximum_fusion.1
  8.7 0.7 copy.86
  9.4 0.0 all-gather.2.cloned.1.call-update
  9.5 1.6 copy.74
  11.1 0.0 copy-done.3
  11.1 1.5 copy.73
  12.6 1.6 copy.83
  14.2 2.4 copy.77
  16.6 0.3 fusion.18
  16.9 1.6 fusion.16
  18.5 0.3 fusion.20
  18.8 28.2 %all-reduce = (f32[1024]{0:T(1024)S(1)}, f32[1024]{0:T(1024)S(1)}, f32[1024]{0:T(1024)S(1)}) all-reduce(f32[1024]{0:T(1024)S(1)} %fusion.16, f32[1024]{0:T(1024)S(1)} %fusion.18, f32[1024]{0:T(1024)S(1)} %fusion.20), channel_id=1, replica_groups=mesh['req'=32,'tp'=8] {'tp'}, use_global_device_ids=true, to_apply=%region_1.0 | all-reduce | flops 3072 | bytes 24576 | tf_op jit(solution)/shard_map/psum | solution.py:98
  47.1 0.0 copy-start.1
  47.1 0.3 fusion.67
  47.4 1.0 copy-done.1
  48.4 1.7 pad_maximum_fusion
  50.1 7.5 %copy.98 = bf16[1024,2,640]{2,1,0:T(2,128)(2,1)} copy(bf16[1024,2,640]{0,2,1:T(8,128)(2,1)} %pad_maximum_fusion) | data formatting | bytes 5242880 | tf_op jit(solution)/shard_map/stack | solution.py:120
  57.6 0.0 copy-start.5
  57.6 5.0 reshape.137
  62.6 0.0 copy-done.5
  62.6 0.2 select_reduce_fusion
  62.8 4.9 convolution_convert_fusion
  67.6 6.8 %reshape.138 = bf16[1536,2,640]{2,1,0:T(2,128)(2,1)} reshape(bf16[96,20480]{1,0:T(8,128)(2,1)} %convolution_convert_fusion) | data formatting | bytes 7864320 | tf_op jit(solution)/shard_map/reshape | solution.py:122
  74.4 7.9 %all-to-all-start = ((bf16[1536,2,640]{2,1,0:T(2,128)(2,1)}), bf16[1536,2,640]{2,1,0:T(2,128)(2,1)}, u32[]{:S(2)}, u32[]{:S(2)}) async-start(bf16[1536,2,640]{2,1,0:T(2,128)(2,1)} %reshape.138), calls=%async_computation | async-start | bytes 7864320 | tf_op jit(solution)/shard_map/all_to_all | solution.py:123
  82.3 0.0 copy-start.4
  82.4 2.7 fusion.17
  85.7 0.0 copy-done.4
  85.8 1.4 fusion.51
  87.1 0.7 broadcast_compare_fusion.1
  87.8 0.3 fusion.19
  88.1 2.3 fusion
  90.4 2.3 fusion.1
  92.7 0.0 copy-start.2
  92.7 6.9 %fusion.2 = (f32[5,512]{1,0:T(8,128)S(1)}, f32[5,512]{1,0:T(8,128)S(1)}) fusion(f32[5,512,1024]{2,1,0:T(8,128)S(1)} %get-tuple-element.30, f32[5,512]{1,0:T(8,128)S(1)} %broadcast_maximum_fusion.3, pred[512,1024]{1,0:T(8,128)(4,1)S(1)} %get-tuple-element.23, f32[5,512]{1,0:T(8,128)S(1)} %broadcast_maximum_fusion.2, f32[5,512,1024]{2,1,0:T(8,128)S(1)} %get-tuple-element.28, ...), kind=kLoop, calls=%fused_computation.7 | loop fusion | flops 26209280 | bytes 22061056 | tf_op jit(solution)/shard_map/reduce_sum | solution.py:38
  99.7 0.0 copy-done.2
  99.7 3.3 divide_convert_fusion.3
  103.0 3.3 divide_convert_fusion.2
  106.3 0.1 maximum_bitcast_fusion
  106.4 1.4 copy.82
  107.8 2.4 copy.99
  110.3 0.3 fusion.21
  110.6 0.1 fusion.50
  110.7 24.5 %all-to-all-done = bf16[1536,2,640]{2,1,0:T(2,128)(2,1)} async-done(((bf16[1536,2,640]{2,1,0:T(2,128)(2,1)}), bf16[1536,2,640]{2,1,0:T(2,128)(2,1)}, u32[]{:S(2)}, u32[]{:S(2)}) %all-to-all-start) | async-done | bytes 3932192 | tf_op jit(solution)/shard_map/all_to_all | solution.py:123
  135.2 344.2 %all-gather.2.cloned.1.call-done = bf16[1024,2,5120]{2,1,0:T(2,128)(2,1)} async-done(((bf16[4,2,5120]{2,1,0:T(2,128)(2,1)}), bf16[1024,2,5120]{2,1,0:T(2,128)(2,1)}) %all-gather.2.cloned.1.call-update) | async-done | bytes 20971536 | tf_op jit(solution)/shard_map/all_gather | solution.py:130
  479.4 7.7 %constant_dynamic-slice_fusion = (bf16[512,1,640]{2,1,0:T(2,128)(2,1)}, bf16[512,1,640]{2,1,0:T(2,128)(2,1)S(1)}) fusion(bf16[1024,2,5120]{2,1,0:T(2,128)(2,1)} %all-gather.2.cloned.1.call-done, s32[]{:T(128)S(6)} %select_n.37, s32[]{:T(128)S(6)} %select_n.39, s32[]{:T(128)S(6)} %add.45), kind=kLoop, calls=%fused_computation.69 | loop fusion | bytes 2621452 | tf_op jit(solution)/shard_map/slice | solution.py:75
  487.1 2.5 copy.118
  489.7 3.2 multiply_reduce_fusion.1
  492.9 1.0 copy.119
  493.9 0.0 copy-start
  493.9 0.9 multiply_reduce_fusion
  494.8 1.6 copy-done
  496.3 0.9 fusion.12
  497.2 1.6 divide_convert_fusion.1
  498.8 0.9 fusion.14
  499.7 1.6 divide_convert_fusion
  501.3 0.1 maximum_bitcast_fusion.1
  501.4 0.6 copy.96
  502.0 1.4 copy.100
  503.5 7.5 %copy.124 = bf16[1536,2,640]{2,1,0:T(2,128)(2,1)} copy(bf16[1536,2,640]{2,1,0:T(2,128)(2,1)} %all-to-all-done) | data formatting | bytes 7864320
  (11 shorter events, 0.1 us)
Async XLA Ops:
  7.2 3.9 copy-start.3
  7.2 472.2 %all-gather.2.cloned.1.call-start = ((), (), s32[]{:S(2)}) async-start(), calls=%async_computation.1 | async-start | bytes 21053440 | tf_op jit(solution)/shard_map/all_gather | solution.py:130
  47.1 1.3 copy-start.1
  57.6 5.0 copy-start.5
  74.4 60.8 %all-to-all-start = ((bf16[1536,2,640]{2,1,0:T(2,128)(2,1)}), bf16[1536,2,640]{2,1,0:T(2,128)(2,1)}, u32[]{:S(2)}, u32[]{:S(2)}) async-start(bf16[1536,2,640]{2,1,0:T(2,128)(2,1)} %reshape.138), calls=%async_computation | async-start | bytes 7864320 | tf_op jit(solution)/shard_map/all_to_all | solution.py:123
  82.3 3.4 copy-start.4
  92.7 7.0 %copy-start.2 = (bf16[1024,640]{0,1:T(8,128)(2,1)S(1)}, bf16[1024,640]{0,1:T(8,128)(2,1)}, u32[]{:S(2)}) copy-start(bf16[1024,640]{0,1:T(8,128)(2,1)} %copy.77) | copy-start | bytes 3932164
  493.9 2.5 copy-start
Sparse Core Ops, SparseCore 0:
  9.9 469.4 all-gather.1
where the time goes:
time: 519 us; the launch traced here: 518 us
  waiting for transfers between devices  369 us (71%)
  local copies, waits for them, and re-layouts  57 us (11%)
  blocking collectives  28.2 us (5%)
  matrix products  23.3 us (4%)
  other arithmetic  17.7 us (3%)
  between operations  15 us (3%)
  starting transfers between devices  7.92 us (2%)
    all_gather x1, waiting for transfers between devices, per_device(): gathered = lax.all_gather(text_ready, ('req', 'tp'), axis=0, tiled=True)  344 us
    psum x1, blocking collectives, per_device(): lax.psum((square_sums(queries), square_sums(keys), square_sums(cross_quer...  28.2 us
    unnamed x22, local copies, waits for them, and re-layouts  24.6 us
    all_to_all x1, waiting for transfers between devices, per_device(): lax.all_to_all(outgoing, 'req', split_axis=0, concat_axis=0, tiled=True)  24.5 us
  transfers between devices with their start and end apart: 2, of which 2 were waited for; matrix products, arithmetic and copies ran while one was open for 12% of the time, Pallas kernels for 0%

commit v1 on v0

--- a/solution.py
+++ b/solution.py
@@ -127,7 +127,13 @@
     self_out = self_attention(query_heads, key_heads, value_heads, segment_ids[0])
     cross_heads = cross_hat.reshape(stream, heads_dev, HEAD)
     prompt_start = prompt_of[0] * TEXT
-    gathered = lax.all_gather(text_ready, ("req", "tp"), axis=0, tiled=True)
+    follow_the_ways = lambda vals: jnp.concatenate(
+        jax.lax.all_to_all(
+            jnp.stack([vals] * jax.lax.axis_size(("req", "tp")), 0), ("req", "tp"), 0, 0
+        ),
+        0,
+    )
+    gathered = follow_the_ways(text_ready)
     prompt_rows = lax.dynamic_slice_in_dim(gathered, prompt_start, TEXT, 0)
     head_start = lax.axis_index("tp") * width_dev
     prompt_rows = lax.dynamic_slice_in_dim(prompt_rows, head_start, width_dev, 2)

time: 519 us -> 644 us (1.24)
  waiting for transfers between devices: 369 us -> 473 us
  starting transfers between devices: 7.92 us -> 29.4 us
  between operations: 15 us -> 1.61 us
  local copies, waits for them, and re-layouts: 57 us -> 66 us
    all_to_all x0 -> x1, waiting for transfers between devices: none -> 426 us  [per_device(): jax.lax.all_to_all(jnp.stack([vals] * jax.lax.axis_size(('req', 'tp')), 0...]
    all_gather x1 -> x0, waiting for transfers between devices: 344 us -> none  [per_device(): gathered = lax.all_gather(text_ready, ('req', 'tp'), axis=0, tiled=True)]
    all_to_all x1, waiting for transfers between devices: 24.5 us -> 46.9 us  [per_device(): lax.all_to_all(outgoing, 'req', split_axis=0, concat_axis=0, tiled=True)]
    all_to_all x0 -> x1, starting transfers between devices: none -> 21.4 us  [per_device(): jax.lax.all_to_all(jnp.stack([vals] * jax.lax.axis_size(('req', 'tp')), 0...]
    another operation x1, local copies, waits for them, and re-layouts: 0.69 us -> 12.6 us  [per_device(): jnp.stack([vals] * jax.lax.axis_size(('req', 'tp')), 0)]
    unnamed x22 -> x23, local copies, waits for them, and re-layouts: 24.6 us -> 22.2 us
  transfers between devices with their start and end apart: 2 -> 2, of which waited for: 2 -> 2; matrix products, arithmetic and copies ran while one was open for 12% -> 4% of each run, Pallas kernels for 0% -> 0%
where the time goes in v1:
time: 644 us; the launch traced here: 638 us
  waiting for transfers between devices  473 us (73%)
  local copies, waits for them, and re-layouts  66 us (10%)
  starting transfers between devices  29.4 us (5%)
  blocking collectives  28 us (4%)
  matrix products  24.4 us (4%)
  other arithmetic  15.5 us (2%)
    all_to_all x1, waiting for transfers between devices, per_device(): jax.lax.all_to_all(jnp.stack([vals] * jax.lax.axis_size(('req', 'tp')), 0...  426 us
    all_to_all x1, waiting for transfers between devices, per_device(): lax.all_to_all(outgoing, 'req', split_axis=0, concat_axis=0, tiled=True)  46.9 us
    psum x1, blocking collectives, per_device(): lax.psum((square_sums(queries), square_sums(keys), square_sums(cross_quer...  28 us
    unnamed x23, local copies, waits for them, and re-layouts  22.2 us
    all_to_all x1, starting transfers between devices, per_device(): jax.lax.all_to_all(jnp.stack([vals] * jax.lax.axis_size(('req', 'tp')), 0...  21.4 us
  transfers between devices with their start and end apart: 2, of which 2 were waited for; matrix products, arithmetic and copies ran while one was open for 4% of the time, Pallas kernels for 0%

profile of v1, /device:TPU:64, one launch (start us, length us, event | category | flops | bytes accessed | tf_op | source)
XLA Modules:
  0.0 637.5 jit_solution(2879532188866976282)
XLA Ops:
  0.6 1.6 copy.69
  2.2 0.3 fusion.18
  2.5 1.6 copy.68
  4.2 0.0 copy-start.1
  4.2 1.0 copy-done.1
  5.2 0.3 fusion.16
  5.5 1.6 copy.78
  7.1 0.3 fusion.20
  7.4 28.0 %all-reduce = (f32[1024]{0:T(1024)S(1)}, f32[1024]{0:T(1024)S(1)}, f32[1024]{0:T(1024)S(1)}) all-reduce(f32[1024]{0:T(1024)S(1)} %fusion.16, f32[1024]{0:T(1024)S(1)} %fusion.18, f32[1024]{0:T(1024)S(1)} %fusion.20), channel_id=1, replica_groups=mesh['req'=32,'tp'=8] {'tp'}, use_global_device_ids=true, to_apply=%region_1.0 | all-reduce | flops 3072 | bytes 24576 | tf_op jit(solution)/shard_map/psum | solution.py:98
  35.5 2.4 copy.72
  37.9 0.0 copy-start.2
  37.9 0.3 fusion.64
  38.2 1.0 copy-done.2
  39.2 1.7 pad_maximum_fusion
  40.9 7.5 %copy.91 = bf16[1024,2,640]{2,1,0:T(2,128)(2,1)} copy(bf16[1024,2,640]{0,2,1:T(8,128)(2,1)} %pad_maximum_fusion) | data formatting | bytes 5242880 | tf_op jit(solution)/shard_map/stack | solution.py:120
  48.5 4.9 reshape.143
  53.4 0.0 copy-done.7
  53.4 0.2 select_reduce_fusion
  53.6 4.8 convolution_convert_fusion
  58.4 6.7 %reshape.144 = bf16[1536,2,640]{2,1,0:T(2,128)(2,1)} reshape(bf16[96,20480]{1,0:T(8,128)(2,1)} %convolution_convert_fusion) | data formatting | bytes 7864320 | tf_op jit(solution)/shard_map/reshape | solution.py:122
  65.1 8.0 %all-to-all-start.1 = ((bf16[1536,2,640]{2,1,0:T(2,128)(2,1)}), bf16[1536,2,640]{2,1,0:T(2,128)(2,1)}, u32[]{:S(2)}, u32[]{:S(2)}) async-start(bf16[1536,2,640]{2,1,0:T(2,128)(2,1)} %reshape.144), calls=%async_computation.1 | async-start | bytes 7864320 | tf_op jit(solution)/shard_map/all_to_all | solution.py:123
  73.2 0.0 copy-done.5
  73.2 0.1 slice.53
  73.3 0.2 multiply_reduce_fusion.2
  73.5 0.1 multiply_convert_fusion
  73.6 0.2 pad_maximum_fusion.1
  73.8 46.9 %all-to-all-done.1 = bf16[1536,2,640]{2,1,0:T(2,128)(2,1)} async-done(((bf16[1536,2,640]{2,1,0:T(2,128)(2,1)}), bf16[1536,2,640]{2,1,0:T(2,128)(2,1)}, u32[]{:S(2)}, u32[]{:S(2)}) %all-to-all-start.1) | async-done | bytes 3932192 | tf_op jit(solution)/shard_map/all_to_all | solution.py:123
  120.7 12.6 %stack.11 = bf16[256,4,2,5120]{3,2,1,0:T(2,128)(2,1)} broadcast(bf16[4,2,5120]{2,1,0:T(2,128)(2,1)S(1)} %pad_maximum_fusion.1), dimensions={1,2,3} | broadcast | bytes 21053440 | tf_op jit(solution)/shard_map/stack | solution.py:132
  133.3 21.4 %all-to-all-start = ((bf16[256,4,2,5120]{3,2,1,0:T(2,128)(2,1)}), bf16[256,4,2,5120]{3,2,1,0:T(2,128)(2,1)}, u32[]{:S(2)}, u32[]{:S(2)}) async-start(bf16[256,4,2,5120]{3,2,1,0:T(2,128)(2,1)} %stack.11), calls=%async_computation | async-start | bytes 41943040 | tf_op jit(solution)/shard_map/all_to_all | solution.py:131
  155.3 0.0 copy-done.6
  155.4 1.6 fusion.17
  157.0 0.1 fusion.49
  157.1 0.7 broadcast_compare_fusion.1
  157.8 0.3 fusion.19
  158.1 2.3 fusion
  160.4 2.3 fusion.1
  162.7 0.0 copy-start.3
  162.7 6.9 %fusion.2 = (f32[5,512]{1,0:T(8,128)S(1)}, f32[5,512]{1,0:T(8,128)S(1)}) fusion(f32[5,512,1024]{2,1,0:T(8,128)S(1)} %get-tuple-element.28, f32[5,512]{1,0:T(8,128)S(1)} %broadcast_maximum_fusion.3, pred[512,1024]{1,0:T(8,128)(4,1)S(1)} %get-tuple-element.21, f32[5,512]{1,0:T(8,128)S(1)} %broadcast_maximum_fusion.2, f32[5,512,1024]{2,1,0:T(8,128)S(1)} %get-tuple-element.26, ...), kind=kLoop, calls=%fused_computation.7 | loop fusion | flops 26209280 | bytes 22061056 | tf_op jit(solution)/shard_map/reduce_sum | solution.py:38
  169.7 0.0 copy-done.3
  169.7 3.3 divide_convert_fusion.3
  173.0 3.3 divide_convert_fusion.2
  176.3 0.1 maximum_bitcast_fusion
  176.4 1.4 copy.77
  177.8 2.4 copy.92
  180.2 0.3 fusion.21
  180.6 1.1 fusion.48
  181.7 425.7 %all-to-all-done = bf16[256,4,2,5120]{3,2,1,0:T(2,128)(2,1)} async-done(((bf16[256,4,2,5120]{3,2,1,0:T(2,128)(2,1)}), bf16[256,4,2,5120]{3,2,1,0:T(2,128)(2,1)}, u32[]{:S(2)}, u32[]{:S(2)}) %all-to-all-start) | async-done | bytes 20971552 | tf_op jit(solution)/shard_map/all_to_all | solution.py:131
  607.4 6.7 %constant_dynamic-slice_fusion = (bf16[512,1,640]{2,1,0:T(2,128)(2,1)S(1)}, bf16[512,1,640]{2,1,0:T(2,128)(2,1)S(1)}) fusion(bf16[1024,2,5120]{2,1,0:T(2,128)(2,1)} %bitcast.10, s32[]{:T(128)S(6)} %select_n.37, s32[]{:T(128)S(6)} %select_n.39, s32[]{:T(128)S(6)} %add.45), kind=kLoop, calls=%fused_computation.67 | loop fusion | bytes 2621452 | tf_op jit(solution)/shard_map/slice | solution.py:75
  614.1 1.0 copy.79
  615.1 0.0 copy-start.4
  615.1 4.4 multiply_reduce_fusion.1
  619.5 1.0 copy.82
  620.4 0.0 copy-done.4
  620.4 0.0 copy-start
  620.4 0.9 multiply_reduce_fusion
  621.4 1.6 copy-done
  622.9 0.9 fusion.12
  623.8 1.6 divide_convert_fusion.1
  625.4 0.9 fusion.14
  626.3 1.6 divide_convert_fusion
  627.9 0.1 maximum_bitcast_fusion.1
  628.0 0.6 copy.89
  628.6 1.4 copy.93
  630.0 7.5 %copy.110 = bf16[1536,2,640]{2,1,0:T(2,128)(2,1)} copy(bf16[1536,2,640]{2,1,0:T(2,128)(2,1)} %all-to-all-done.1) | data formatting | bytes 7864320
  (13 shorter events, 0.1 us)
Async XLA Ops:
  4.2 1.1 copy-start.1
  37.9 1.3 copy-start.2
  48.5 4.9 copy-start.7
  65.1 8.0 %copy-start.5 = (bf16[4,2,5120]{2,1,0:T(2,128)(2,1)S(1)}, bf16[4,2,5120]{2,1,0:T(2,128)(2,1)}, u32[]{:S(2)}) copy-start(bf16[4,2,5120]{2,1,0:T(2,128)(2,1)} %param.12) | copy-start | bytes 245764
  65.1 55.6 %all-to-all-start.1 = ((bf16[1536,2,640]{2,1,0:T(2,128)(2,1)}), bf16[1536,2,640]{2,1,0:T(2,128)(2,1)}, u32[]{:S(2)}, u32[]{:S(2)}) async-start(bf16[1536,2,640]{2,1,0:T(2,128)(2,1)} %reshape.144), calls=%async_computation.1 | async-start | bytes 7864320 | tf_op jit(solution)/shard_map/all_to_all | solution.py:123
  133.3 22.0 %copy-start.6 = (s32[1,1024]{1,0:T(1,128)S(1)}, s32[1,1024]{1,0:T(1,128)}, u32[]{:S(2)}) copy-start(s32[1,1024]{1,0:T(1,128)} %param.13) | copy-start | bytes 12292
  133.3 474.1 %all-to-all-start = ((bf16[256,4,2,5120]{3,2,1,0:T(2,128)(2,1)}), bf16[256,4,2,5120]{3,2,1,0:T(2,128)(2,1)}, u32[]{:S(2)}, u32[]{:S(2)}) async-start(bf16[256,4,2,5120]{3,2,1,0:T(2,128)(2,1)} %stack.11), calls=%async_computation | async-start | bytes 41943040 | tf_op jit(solution)/shard_map/all_to_all | solution.py:131
  162.7 7.0 %copy-start.3 = (bf16[1024,640]{0,1:T(8,128)(2,1)S(1)}, bf16[1024,640]{0,1:T(8,128)(2,1)}, u32[]{:S(2)}) copy-start(bf16[1024,640]{0,1:T(8,128)(2,1)} %copy.72) | copy-start | bytes 3932164
  615.1 5.3 copy-start.4
  620.4 2.5 copy-start
